TPU v7x, 512 devices: a whole 4x8x8 slice. The times are simulated.
512 devices in a mesh: wide: 64 (over y, x, core), narrow: 8 (over z).
Axes of the slice: x: 4, y: 8, z: 8, core: 2. Of those that a mesh axis runs over, the one named last changes fastest.
Arguments:
- matrix_slab: float32 [16, 4194304], P(None, ('wide', 'narrow')), may hold values from -6 to 6
- row_signs: int32 [4194304], P(('wide', 'narrow')), may hold values from -1 to 1, as said below
- sample_rows: int32 [524288], P(('wide', 'narrow')), may hold values from 0 to 7, as said below
Outputs:
- sketch: float32 [16, 524288], P(None, ('wide', 'narrow'))
- sketch_gram: float32 [16, 16], replicated
Inputs may be any that keep to these rules, and one draw needn't show every extreme that they name: `row_signs`: each entry is +1 or -1. `sample_rows`: entry k is the offset of the k-th sampled row inside the run of 8 rows that starts at k * 8.
All inputs are finite; a program needn't handle non-finite values.
Results may differ from a plain program's by a relative error of at most 0.00013.
Values sent between devices are 32-bit elements; how exact they have to be, the bound alone decides.
A program may use at most 64 MiB of HBM per device.

v0:
```python
import math
import jax
import jax.numpy as jnp
from jax import lax
from jax.sharding import PartitionSpec as P


def from_partner(value, axis, apart):
    mask = 2**apart
    pairs = [(source, source ^ mask) for source in range(lax.axis_size(axis))]
    return lax.ppermute(value, axis, pairs)


def sylvester(order_size):
    series = lax.iota(jnp.int32, order_size)
    common_bits = series[:, None] & series[None, :]
    parity = jnp.zeros_like(common_bits)
    for bit_pos in range(order_size.bit_length() - 1):
        parity = parity ^ common_bits >> bit_pos & 1
    return (1 - 2 * parity).astype(jnp.float32)


def narrow_section(values):
    axis_width = lax.axis_size("narrow")
    position = lax.axis_index("narrow")
    for bit_pos in range(axis_width.bit_length() - 1):
        partner = from_partner(values, "narrow", bit_pos)
        own_bit = position >> bit_pos & 1
        values = jnp.where(own_bit == 0, values + partner, partner - values)
    return values


def pick_samples(values, sample_rows):
    sample_count = sample_rows.shape[0]
    run_length = values.shape[1] // sample_count
    local_rows = lax.iota(jnp.int32, sample_count) * run_length + sample_rows
    return jnp.take(values, local_rows, axis=1)


def wide_section(values, sample_rows):
    axis_width = lax.axis_size("wide")
    columns, row_count = values.shape
    hadamard = sylvester(axis_width)
    blocked = values.reshape(columns, axis_width, row_count // axis_width)
    mixed_rows = jnp.einsum(
        "ms,csr->cmr",
        hadamard,
        lax.all_to_all(blocked, "wide", split_axis=1, concat_axis=1, tiled=True),
        precision=lax.Precision.HIGHEST,
    )
    result = lax.all_to_all(mixed_rows, "wide", split_axis=1, concat_axis=1, tiled=True)
    result = result.reshape(columns, row_count)
    return pick_samples(result, sample_rows)


def shards(matrix_slab, row_signs, sample_rows):
    values = matrix_slab * row_signs.astype(jnp.float32)[None, :]
    columns, row_count = values.shape
    inner_table = sylvester(128)
    outer_table = sylvester(row_count // 128)
    tiles = values.reshape(columns, row_count // 128, 128)
    tiles = jnp.einsum("cqt,ts->cqs", tiles, inner_table, precision=lax.Precision.HIGHEST)
    tiles = jnp.einsum("pq,cqs->cps", outer_table, tiles, precision=lax.Precision.HIGHEST)
    values = tiles.reshape(columns, row_count)
    values = narrow_section(values)
    picked_rows = wide_section(values, sample_rows)
    devices_all = lax.axis_size("wide") * lax.axis_size("narrow")
    sketch = picked_rows * jnp.float32(1.0 / math.sqrt(row_count * devices_all))
    sample_count = sample_rows.shape[0]
    partial_gram = jnp.dot(
        sketch, sketch.T, precision=lax.Precision.HIGHEST, preferred_element_type=jnp.float32
    ) / jnp.float32(sample_count * devices_all)
    sketch_gram = lax.psum(partial_gram, ("wide", "narrow"))
    return (sketch, sketch_gram)


def solution(mesh):
    in_specs = (P(None, ("wide", "narrow")), P(("wide", "narrow")), P(("wide", "narrow")))
    out_specs = (P(None, ("wide", "narrow")), P())
    return jax.shard_map(shards, mesh=mesh, in_specs=in_specs, out_specs=out_specs, check_vma=False)
```

profile of v0, /device:TPU:1, one launch (start us, length us, event | category | flops | bytes accessed | tf_op | source)
XLA Modules:
  0.0 241.7 jit_solution(14482409116508778793)
XLA Ops:
  0.6 0.8 convert_element_type.12
  1.4 1.1 multiply_bitcast_fusion
  2.5 0.1 copy.17
  2.6 0.6 fusion.5
  3.2 0.6 fusion.34
  3.8 0.3 copy.25
  4.1 4.8 %collective-permute-start = (f32[16,8192]{1,0:T(8,128)S(1)}, f32[16,8192]{1,0:T(8,128)S(1)}, u32[]{:S(2)}, u32[]{:S(2)}) collective-permute-start(f32[16,8192]{1,0:T(8,128)S(1)} %bitcast.34), channel_id=1, source_target_pairs={{0,1},{1,0},{2,3},{3,2},{4,5},{5,4},{6,7},{7,6},{8,9},{9,8},{10,11... | collective-permute-start | bytes 1572872 | tf_op jit(solution)/shard_map/ppermute | solution.py:11
  9.0 0.0 copy-start
  9.0 7.5 %collective-permute-done = f32[16,8192]{1,0:T(8,128)S(1)} collective-permute-done((f32[16,8192]{1,0:T(8,128)S(1)}, f32[16,8192]{1,0:T(8,128)S(1)}, u32[]{:S(2)}, u32[]{:S(2)}) %collective-permute-start) | collective-permute-done | bytes 524320 | tf_op jit(solution)/shard_map/ppermute | solution.py:11
  16.5 0.3 subtract_select_fusion.1
  16.8 9.9 %collective-permute-start.1 = (f32[16,8192]{1,0:T(8,128)S(1)}, f32[16,8192]{1,0:T(8,128)S(1)}, u32[]{:S(2)}, u32[]{:S(2)}) collective-permute-start(f32[16,8192]{1,0:T(8,128)S(1)} %subtract_select_fusion.1), channel_id=1, source_target_pairs={{0,2},{1,3},{2,0},{3,1},{4,6},{5,7},{6,4},{7,5},{8,10},{9,11},{10,... | collective-permute-start | bytes 1572872 | tf_op jit(solution)/shard_map/ppermute | solution.py:11
  26.8 22.7 %collective-permute-done.1 = f32[16,8192]{1,0:T(8,128)S(1)} collective-permute-done((f32[16,8192]{1,0:T(8,128)S(1)}, f32[16,8192]{1,0:T(8,128)S(1)}, u32[]{:S(2)}, u32[]{:S(2)}) %collective-permute-start.1) | collective-permute-done | bytes 524320 | tf_op jit(solution)/shard_map/ppermute | solution.py:11
  49.5 0.1 subtract_select_fusion
  49.5 8.1 %collective-permute-start.2 = (f32[16,8192]{1,0:T(8,128)S(1)}, f32[16,8192]{1,0:T(8,128)S(1)}, u32[]{:S(2)}, u32[]{:S(2)}) collective-permute-start(f32[16,8192]{1,0:T(8,128)S(1)} %subtract_select_fusion), channel_id=1, source_target_pairs={{0,4},{1,5},{2,6},{3,7},{4,0},{5,1},{6,2},{7,3},{8,12},{9,13},{10,... | collective-permute-start | bytes 1572872 | tf_op jit(solution)/shard_map/ppermute | solution.py:11
  57.6 22.1 %collective-permute-done.2 = f32[16,8192]{1,0:T(8,128)S(1)} collective-permute-done((f32[16,8192]{1,0:T(8,128)S(1)}, f32[16,8192]{1,0:T(8,128)S(1)}, u32[]{:S(2)}, u32[]{:S(2)}) %collective-permute-start.2) | collective-permute-done | bytes 524320 | tf_op jit(solution)/shard_map/ppermute | solution.py:11
  79.7 0.1 copy_bitcast_fusion.1
  79.7 29.8 %all_to_all.10 = f32[16,64,128]{2,0,1:T(8,128)S(1)} all-to-all(f32[16,64,128]{2,0,1:T(8,128)S(1)} %copy_bitcast_fusion.1), channel_id=1, replica_groups=mesh['wide'=64,'narrow'=8] {'wide'}, dimensions={1} | all-to-all | bytes 1048576 | tf_op jit(solution)/shard_map/all_to_all | solution.py:48
  109.5 0.8 convolution_bitcast_fusion
  110.3 1.1 copy.13
  111.4 5.7 %all-to-all-start.1 = ((f32[16,64,128]{2,0,1:T(8,128)}), f32[16,64,128]{2,0,1:T(8,128)S(1)}, u32[]{:S(2)}, u32[]{:S(2)}) async-start(f32[16,64,128]{2,0,1:T(8,128)} %copy.13), calls=%async_computation.1 | async-start | bytes 1048576 | tf_op jit(solution)/shard_map/all_to_all | solution.py:51
  117.1 0.0 copy-done
  117.2 17.7 %all-to-all-done.1 = f32[16,64,128]{2,0,1:T(8,128)S(1)} async-done(((f32[16,64,128]{2,0,1:T(8,128)}), f32[16,64,128]{2,0,1:T(8,128)S(1)}, u32[]{:S(2)}, u32[]{:S(2)}) %all-to-all-start.1) | async-done | bytes 524320 | tf_op jit(solution)/shard_map/all_to_all | solution.py:51
  134.9 2.6 %copy.14 = f32[16,64,128]{0,2,1:T(8,128)} copy(f32[16,64,128]{2,0,1:T(8,128)S(1)} %all-to-all-done.1) | data formatting | bytes 1048576 | tf_op jit(solution)/shard_map/all_to_all | solution.py:51
  137.5 5.0 %gather_fusion = f32[1024,16]{1,0:T(8,128)S(1)} fusion(f32[16,8192]{0,1:T(8,128)} %bitcast.30, s32[1024]{0:T(1024)S(1)} %fusion.45), kind=kCustom, calls=%fused_computation | custom fusion | bytes 135168 | tf_op jit(solution)/shard_map/jit(_take)/gather | solution.py:37
  142.4 0.2 fusion.1
  142.7 1.3 convolution_multiply_fusion
  143.9 0.8 copy.15
  144.7 97.0 %psum.7 = f32[16,16]{1,0:T(8,128)} all-reduce(f32[16,16]{1,0:T(8,128)S(1)} %convolution_multiply_fusion), channel_id=1, replica_groups=mesh['wide'=64,'narrow'=8] {'wide','narrow'}, use_global_device_ids=true, to_apply=%region_0.1 | all-reduce | flops 256 | bytes 2048 | tf_op jit(solution)/shard_map/psum | solution.py:73
  (2 shorter events, 0.0 us)
Async XLA Ops:
  4.1 12.3 %collective-permute-start = (f32[16,8192]{1,0:T(8,128)S(1)}, f32[16,8192]{1,0:T(8,128)S(1)}, u32[]{:S(2)}, u32[]{:S(2)}) collective-permute-start(f32[16,8192]{1,0:T(8,128)S(1)} %bitcast.34), channel_id=1, source_target_pairs={{0,1},{1,0},{2,3},{3,2},{4,5},{5,4},{6,7},{7,6},{8,9},{9,8},{10,11... | collective-permute-start | bytes 1572872 | tf_op jit(solution)/shard_map/ppermute | solution.py:11
  9.0 108.1 %copy-start = (s32[1024]{0:T(1024)S(1)}, s32[1024]{0:T(1024)}, u32[]{:S(2)}) copy-start(s32[1024]{0:T(1024)} %param.5) | copy-start | bytes 12292
  16.8 32.6 %collective-permute-start.1 = (f32[16,8192]{1,0:T(8,128)S(1)}, f32[16,8192]{1,0:T(8,128)S(1)}, u32[]{:S(2)}, u32[]{:S(2)}) collective-permute-start(f32[16,8192]{1,0:T(8,128)S(1)} %subtract_select_fusion.1), channel_id=1, source_target_pairs={{0,2},{1,3},{2,0},{3,1},{4,6},{5,7},{6,4},{7,5},{8,10},{9,11},{10,... | collective-permute-start | bytes 1572872 | tf_op jit(solution)/shard_map/ppermute | solution.py:11
  49.5 30.2 %collective-permute-start.2 = (f32[16,8192]{1,0:T(8,128)S(1)}, f32[16,8192]{1,0:T(8,128)S(1)}, u32[]{:S(2)}, u32[]{:S(2)}) collective-permute-start(f32[16,8192]{1,0:T(8,128)S(1)} %subtract_select_fusion), channel_id=1, source_target_pairs={{0,4},{1,5},{2,6},{3,7},{4,0},{5,1},{6,2},{7,3},{8,12},{9,13},{10,... | collective-permute-start | bytes 1572872 | tf_op jit(solution)/shard_map/ppermute | solution.py:11
  111.4 23.4 %all-to-all-start.1 = ((f32[16,64,128]{2,0,1:T(8,128)}), f32[16,64,128]{2,0,1:T(8,128)S(1)}, u32[]{:S(2)}, u32[]{:S(2)}) async-start(f32[16,64,128]{2,0,1:T(8,128)} %copy.13), calls=%async_computation.1 | async-start | bytes 1048576 | tf_op jit(solution)/shard_map/all_to_all | solution.py:51
where the time goes:
time: 242 us
  blocking collectives  127 us (52%)
  waiting for transfers between devices  69.9 us (29%)
  starting transfers between devices  28.6 us (12%)
  local copies, waits for them, and re-layouts  9.92 us (4%)
  matrix products  3.23 us (1%)
  other arithmetic  2.51 us (1%)
    psum x1, blocking collectives, shards(): sketch_gram = lax.psum(partial_gram, ('wide', 'narrow'))  97 us
    ppermute x3, waiting for transfers between devices, from_partner(): return lax.ppermute(value, axis, pairs)  52.3 us
    all_to_all x1, blocking collectives, wide_section(): lax.all_to_all(blocked, 'wide', split_axis=1, concat_axis=1, tiled=True)  29.8 us
    ppermute x3, starting transfers between devices, from_partner(): return lax.ppermute(value, axis, pairs)  22.8 us
    all_to_all x1, waiting for transfers between devices, wide_section(): lax.all_to_all(mixed_rows, 'wide', split_axis=1, concat_axis=1, tiled=True)  17.7 us
    all_to_all x1, starting transfers between devices, wide_section(): lax.all_to_all(mixed_rows, 'wide', split_axis=1, concat_axis=1, tiled=True)  5.73 us
    gather x1, local copies, waits for them, and re-layouts, pick_samples(): return jnp.take(values, local_rows, axis=1)  4.99 us
  transfers between devices with their start and end apart: 4, of which 4 were waited for; matrix products, arithmetic and copies ran while one was open for 0% of the time, Pallas kernels for 0%

commit v1 on v0

--- a/solution.py
+++ b/solution.py
@@ -70,7 +70,7 @@
     partial_gram = jnp.dot(
         sketch, sketch.T, precision=lax.Precision.HIGHEST, preferred_element_type=jnp.float32
     ) / jnp.float32(sample_count * devices_all)
-    sketch_gram = lax.psum(partial_gram, ("wide", "narrow"))
+    sketch_gram = jnp.sum(lax.all_gather(partial_gram, ("wide", "narrow")), axis=0)
     return (sketch, sketch_gram)
 
 

time: 242 us -> 232 us (0.959); the launches traced: 242 us -> 229 us
  blocking collectives: 127 us -> 111 us
  other arithmetic: 2.51 us -> 5.85 us
    psum x1 -> x0, blocking collectives: 97 us -> none  [shards(): sketch_gram = lax.psum(partial_gram, ('wide', 'narrow'))]
    all_gather x0 -> x1, blocking collectives: none -> 80.9 us  [shards(): lax.all_gather(partial_gram, ('wide', 'narrow'))]
    reduce_sum x0 -> x1, other arithmetic: none -> 3.34 us  [shards(): jnp.sum(lax.all_gather(partial_gram, ('wide', 'narrow')), axis=0)]
where the time goes in v1:
time: 232 us; the launch traced here: 229 us
  blocking collectives  111 us (48%)
  waiting for transfers between devices  69.9 us (30%)
  starting transfers between devices  28.6 us (12%)
  local copies, waits for them, and re-layouts  9.92 us (4%)
  other arithmetic  5.85 us (3%)
  matrix products  3.23 us (1%)
    all_gather x1, blocking collectives, shards(): lax.all_gather(partial_gram, ('wide', 'narrow'))  80.9 us
    ppermute x3, waiting for transfers between devices, from_partner(): return lax.ppermute(value, axis, pairs)  52.3 us
    all_to_all x1, blocking collectives, wide_section(): lax.all_to_all(blocked, 'wide', split_axis=1, concat_axis=1, tiled=True)  29.8 us
    ppermute x3, starting transfers between devices, from_partner(): return lax.ppermute(value, axis, pairs)  22.8 us
    all_to_all x1, waiting for transfers between devices, wide_section(): lax.all_to_all(mixed_rows, 'wide', split_axis=1, concat_axis=1, tiled=True)  17.7 us
    all_to_all x1, starting transfers between devices, wide_section(): lax.all_to_all(mixed_rows, 'wide', split_axis=1, concat_axis=1, tiled=True)  5.72 us
    gather x1, local copies, waits for them, and re-layouts, pick_samples(): return jnp.take(values, local_rows, axis=1)  4.99 us
  transfers between devices with their start and end apart: 4, of which 4 were waited for; matrix products, arithmetic and copies ran while one was open for 0% of the time, Pallas kernels for 0%

profile of v1, /device:TPU:1, one launch (start us, length us, event | category | flops | bytes accessed | tf_op | source)
XLA Modules:
  0.0 229.0 jit_solution(980489365838424733)
XLA Ops:
  0.6 0.8 convert_element_type.12
  1.4 1.1 multiply_bitcast_fusion
  2.5 0.1 copy.17
  2.6 0.6 fusion.5
  3.2 0.6 fusion.34
  3.8 0.3 copy.25
  4.1 4.8 %collective-permute-start = (f32[16,8192]{1,0:T(8,128)S(1)}, f32[16,8192]{1,0:T(8,128)S(1)}, u32[]{:S(2)}, u32[]{:S(2)}) collective-permute-start(f32[16,8192]{1,0:T(8,128)S(1)} %bitcast.36), channel_id=1, source_target_pairs={{0,1},{1,0},{2,3},{3,2},{4,5},{5,4},{6,7},{7,6},{8,9},{9,8},{10,11... | collective-permute-start | bytes 1572872 | tf_op jit(solution)/shard_map/ppermute | solution.py:11
  9.0 0.0 copy-start
  9.0 7.5 %collective-permute-done = f32[16,8192]{1,0:T(8,128)S(1)} collective-permute-done((f32[16,8192]{1,0:T(8,128)S(1)}, f32[16,8192]{1,0:T(8,128)S(1)}, u32[]{:S(2)}, u32[]{:S(2)}) %collective-permute-start) | collective-permute-done | bytes 524320 | tf_op jit(solution)/shard_map/ppermute | solution.py:11
  16.5 0.3 subtract_select_fusion.1
  16.8 9.9 %collective-permute-start.1 = (f32[16,8192]{1,0:T(8,128)S(1)}, f32[16,8192]{1,0:T(8,128)S(1)}, u32[]{:S(2)}, u32[]{:S(2)}) collective-permute-start(f32[16,8192]{1,0:T(8,128)S(1)} %subtract_select_fusion.1), channel_id=1, source_target_pairs={{0,2},{1,3},{2,0},{3,1},{4,6},{5,7},{6,4},{7,5},{8,10},{9,11},{10,... | collective-permute-start | bytes 1572872 | tf_op jit(solution)/shard_map/ppermute | solution.py:11
  26.8 22.7 %collective-permute-done.1 = f32[16,8192]{1,0:T(8,128)S(1)} collective-permute-done((f32[16,8192]{1,0:T(8,128)S(1)}, f32[16,8192]{1,0:T(8,128)S(1)}, u32[]{:S(2)}, u32[]{:S(2)}) %collective-permute-start.1) | collective-permute-done | bytes 524320 | tf_op jit(solution)/shard_map/ppermute | solution.py:11
  49.5 0.1 subtract_select_fusion
  49.5 8.1 %collective-permute-start.2 = (f32[16,8192]{1,0:T(8,128)S(1)}, f32[16,8192]{1,0:T(8,128)S(1)}, u32[]{:S(2)}, u32[]{:S(2)}) collective-permute-start(f32[16,8192]{1,0:T(8,128)S(1)} %subtract_select_fusion), channel_id=1, source_target_pairs={{0,4},{1,5},{2,6},{3,7},{4,0},{5,1},{6,2},{7,3},{8,12},{9,13},{10,... | collective-permute-start | bytes 1572872 | tf_op jit(solution)/shard_map/ppermute | solution.py:11
  57.6 22.1 %collective-permute-done.2 = f32[16,8192]{1,0:T(8,128)S(1)} collective-permute-done((f32[16,8192]{1,0:T(8,128)S(1)}, f32[16,8192]{1,0:T(8,128)S(1)}, u32[]{:S(2)}, u32[]{:S(2)}) %collective-permute-start.2) | collective-permute-done | bytes 524320 | tf_op jit(solution)/shard_map/ppermute | solution.py:11
  79.7 0.1 copy_bitcast_fusion.1
  79.7 29.8 %all_to_all.10 = f32[16,64,128]{2,0,1:T(8,128)S(1)} all-to-all(f32[16,64,128]{2,0,1:T(8,128)S(1)} %copy_bitcast_fusion.1), channel_id=1, replica_groups=mesh['wide'=64,'narrow'=8] {'wide'}, dimensions={1} | all-to-all | bytes 1048576 | tf_op jit(solution)/shard_map/all_to_all | solution.py:48
  109.5 0.8 convolution_bitcast_fusion
  110.3 1.1 copy.13
  111.4 5.7 %all-to-all-start.1 = ((f32[16,64,128]{2,0,1:T(8,128)}), f32[16,64,128]{2,0,1:T(8,128)S(1)}, u32[]{:S(2)}, u32[]{:S(2)}) async-start(f32[16,64,128]{2,0,1:T(8,128)} %copy.13), calls=%async_computation.1 | async-start | bytes 1048576 | tf_op jit(solution)/shard_map/all_to_all | solution.py:51
  117.1 0.0 copy-done
  117.2 17.7 %all-to-all-done.1 = f32[16,64,128]{2,0,1:T(8,128)S(1)} async-done(((f32[16,64,128]{2,0,1:T(8,128)}), f32[16,64,128]{2,0,1:T(8,128)S(1)}, u32[]{:S(2)}, u32[]{:S(2)}) %all-to-all-start.1) | async-done | bytes 524320 | tf_op jit(solution)/shard_map/all_to_all | solution.py:51
  134.9 2.6 %copy.14 = f32[16,64,128]{0,2,1:T(8,128)} copy(f32[16,64,128]{2,0,1:T(8,128)S(1)} %all-to-all-done.1) | data formatting | bytes 1048576 | tf_op jit(solution)/shard_map/all_to_all | solution.py:51
  137.5 5.0 %gather_fusion = f32[1024,16]{1,0:T(8,128)S(1)} fusion(f32[16,8192]{0,1:T(8,128)} %bitcast.32, s32[1024]{0:T(1024)S(1)} %fusion.45), kind=kCustom, calls=%fused_computation | custom fusion | bytes 135168 | tf_op jit(solution)/shard_map/jit(_take)/gather | solution.py:37
  142.4 0.2 fusion.1
  142.7 1.3 convolution_multiply_fusion
  143.9 0.8 copy.15
  144.7 80.9 %all-gather = f32[8192,16]{1,0:T(8,128)} all-gather(f32[16,16]{1,0:T(8,128)S(1)} %convolution_multiply_fusion), channel_id=2, replica_groups=mesh['wide'=64,'narrow'=8] {'wide','narrow'}, dimensions={0}, use_global_device_ids=true | all-gather | bytes 525312 | tf_op jit(solution)/shard_map/all_gather | solution.py:73
  225.6 3.3 %reduce_sum.9 = f32[16,16]{1,0:T(8,128)} reduce(f32[512,16,16]{2,1,0:T(8,128)} %bitcast.31, f32[]{:T(128)} %constant.9.clone.1), dimensions={0}, to_apply=%region_0.1 | reduce | flops 130816 | bytes 525316 | tf_op jit(solution)/shard_map/reduce_sum | solution.py:73
  (2 shorter events, 0.0 us)
Async XLA Ops:
  4.1 12.3 %collective-permute-start = (f32[16,8192]{1,0:T(8,128)S(1)}, f32[16,8192]{1,0:T(8,128)S(1)}, u32[]{:S(2)}, u32[]{:S(2)}) collective-permute-start(f32[16,8192]{1,0:T(8,128)S(1)} %bitcast.36), channel_id=1, source_target_pairs={{0,1},{1,0},{2,3},{3,2},{4,5},{5,4},{6,7},{7,6},{8,9},{9,8},{10,11... | collective-permute-start | bytes 1572872 | tf_op jit(solution)/shard_map/ppermute | solution.py:11
  9.0 108.1 %copy-start = (s32[1024]{0:T(1024)S(1)}, s32[1024]{0:T(1024)}, u32[]{:S(2)}) copy-start(s32[1024]{0:T(1024)} %param.5) | copy-start | bytes 12292
  16.8 32.6 %collective-permute-start.1 = (f32[16,8192]{1,0:T(8,128)S(1)}, f32[16,8192]{1,0:T(8,128)S(1)}, u32[]{:S(2)}, u32[]{:S(2)}) collective-permute-start(f32[16,8192]{1,0:T(8,128)S(1)} %subtract_select_fusion.1), channel_id=1, source_target_pairs={{0,2},{1,3},{2,0},{3,1},{4,6},{5,7},{6,4},{7,5},{8,10},{9,11},{10,... | collective-permute-start | bytes 1572872 | tf_op jit(solution)/shard_map/ppermute | solution.py:11
  49.5 30.2 %collective-permute-start.2 = (f32[16,8192]{1,0:T(8,128)S(1)}, f32[16,8192]{1,0:T(8,128)S(1)}, u32[]{:S(2)}, u32[]{:S(2)}) collective-permute-start(f32[16,8192]{1,0:T(8,128)S(1)} %subtract_select_fusion), channel_id=1, source_target_pairs={{0,4},{1,5},{2,6},{3,7},{4,0},{5,1},{6,2},{7,3},{8,12},{9,13},{10,... | collective-permute-start | bytes 1572872 | tf_op jit(solution)/shard_map/ppermute | solution.py:11
  111.4 23.4 %all-to-all-start.1 = ((f32[16,64,128]{2,0,1:T(8,128)}), f32[16,64,128]{2,0,1:T(8,128)S(1)}, u32[]{:S(2)}, u32[]{:S(2)}) async-start(f32[16,64,128]{2,0,1:T(8,128)} %copy.13), calls=%async_computation.1 | async-start | bytes 1048576 | tf_op jit(solution)/shard_map/all_to_all | solution.py:51
